TPU v7x, 32 devices: a whole 2x2x4 slice. The times are simulated.
32 devices in a mesh: fsdp: 16 (over z, y, x), dp: 2 (over core).
Axes of the slice: x: 2, y: 2, z: 4, core: 2. Of those that a mesh axis runs over, the one named last changes fastest.
Arguments:
- grads: bfloat16 [2, 1024, 28672], P('dp', 'fsdp')
- block_slot: int32 [28], replicated, may hold values from 0 to 31, as said below
- left_stats: float32 [32, 1024, 1024], P('fsdp', 'dp')
- right_stats: float32 [32, 1024, 1024], P('fsdp', 'dp')
- left_root: bfloat16 [32, 1024, 1024], P('fsdp', 'dp')
- right_root: bfloat16 [32, 1024, 1024], P('fsdp', 'dp')
Outputs:
- left_new: float32 [32, 1024, 1024], P('fsdp', 'dp')
- right_new: float32 [32, 1024, 1024], P('fsdp', 'dp')
- update: bfloat16 [1024, 28672], P('fsdp')
Inputs may be any that keep to these rules, and one draw needn't show every extreme that they name: The entries of block_slot are distinct. Block b's statistics and roots sit in slot block_slot[b], which belongs to the fsdp device of index block_slot[b] // 2; slots that no block names are empty and their statistics pass through unchanged.
All inputs are finite; a program needn't handle non-finite values.
Results may differ from a plain program's by a relative error of at most 0.015.
Values may be sent and summed in bfloat16 or wider, within the bound.
A program may use at most 128 MiB of HBM per device.

v0:
```python
import jax
import jax.numpy as jnp
from jax import lax
from jax.sharding import PartitionSpec as P

epsilon = 1e-06


def per_device(grads, block_slot, left_stats, right_stats, left_root, right_root):
    local_rows = grads[0]
    row_dev, col_count = local_rows.shape
    block_size = left_stats.shape[2]
    block_count = col_count // block_size
    slot_count = left_stats.shape[0]
    shared_rows = left_stats.shape[1]
    total_slots = slot_count * lax.axis_size("fsdp")
    slot_ids = jnp.arange(total_slots, dtype=jnp.int32)
    matches = block_slot[None, :] == slot_ids[:, None]
    filled = jnp.any(matches, axis=1)
    source = jnp.sum(
        jnp.where(matches, jnp.arange(block_count, dtype=jnp.int32)[None, :], 0), axis=1
    )
    row_start = lax.axis_index("dp") * shared_rows
    band = local_rows.astype(jnp.float32).reshape(row_dev, block_count, block_size)
    shares = lax.psum_scatter(band.astype(jnp.bfloat16), "dp", scatter_dimension=2, tiled=True)
    outgoing = jnp.where(
        filled[None, :, None], jnp.take(shares, source, axis=1), jnp.zeros((), jnp.bfloat16)
    )
    incoming = lax.all_to_all(outgoing, "fsdp", split_axis=1, concat_axis=0, tiled=True)
    gradient = lax.all_gather(incoming, "dp", axis=2, tiled=True)
    own_rows = lax.dynamic_slice_in_dim(gradient, row_start, shared_rows, 0)
    whole_right = lax.all_gather(right_root, "dp", axis=1, tiled=True)
    left_new = left_stats + jnp.einsum(
        "rjc,kjc->jrk", own_rows, gradient, preferred_element_type=jnp.float32
    )
    columns = lax.dynamic_slice_in_dim(gradient, row_start, shared_rows, 2)
    right_new = right_stats + jnp.einsum(
        "rjc,rjk->jck", columns, gradient, preferred_element_type=jnp.float32
    )
    left_applied = jnp.einsum(
        "jrk,kjc->rjc", left_root, gradient, preferred_element_type=jnp.float32
    ).astype(jnp.bfloat16)
    both_applied = jnp.einsum(
        "rjc,jck->rjk", left_applied, whole_right, preferred_element_type=jnp.float32
    )
    squares = lax.psum(jnp.sum(both_applied * both_applied, axis=(0, 2)), "dp")
    factor = lax.rsqrt(squares / (block_size * block_size) + epsilon)
    scaled = (both_applied * factor[None, :, None]).astype(jnp.bfloat16)
    full_rows = lax.all_gather(scaled, "dp", axis=0, tiled=True)
    returned = lax.all_to_all(full_rows, "fsdp", split_axis=0, concat_axis=1, tiled=True)
    update = jnp.take(returned, block_slot, axis=1).reshape(row_dev, col_count)
    return (left_new, right_new, update)


def solution(mesh):
    in_specs = (
        P("dp", "fsdp", None),
        P(),
        P("fsdp", "dp", None),
        P("fsdp", "dp", None),
        P("fsdp", "dp", None),
        P("fsdp", "dp", None),
    )
    out_specs = (P("fsdp", "dp", None), P("fsdp", "dp", None), P("fsdp", None))
    return jax.shard_map(
        per_device, mesh=mesh, in_specs=in_specs, out_specs=out_specs, check_vma=False
    )
```

profile of v0, /device:TPU:14, one launch (start us, length us, event | category | flops | bytes accessed | tf_op | source)
XLA Modules:
  0.0 272.9 jit_solution(7911280126792472011)
XLA Ops:
  7.2 0.0 copy-start
  7.2 0.0 reduce-scatter.2.cloned.1.call-start
  7.2 5.7 %squeeze.3 = bf16[64,28,1024]{2,1,0:T(8,128)(2,1)} reshape(bf16[1,64,28672]{2,1,0:T(8,128)(2,1)} %param.6) | data formatting | bytes 7340032 | tf_op jit(solution)/shard_map/squeeze | solution.py:10
  12.9 6.0 %copy.31 = bf16[64,28,1024]{2,0,1:T(8,128)(2,1)} copy(bf16[64,28,1024]{2,1,0:T(8,128)(2,1)} %squeeze.3) | data formatting | bytes 7340032 | tf_op jit(solution)/shard_map/squeeze | solution.py:10
  19.0 0.0 copy-start.4
  19.0 0.0 reduce-scatter.2.cloned.1.call-update
  19.0 0.0 all-gather.6.cloned.1.call-start
  19.0 0.7 all-gather.6.cloned.1.call-update
  19.8 0.0 all-gather.4.cloned.1.call-start
  19.8 0.0 copy-done.4
  19.8 0.1 select_reduce_fusion
  19.9 0.1 fusion.16
  20.1 12.2 %reduce-scatter.2.cloned.1.call-done = bf16[64,28,512]{2,0,1:T(8,128)(2,1)} async-done(((bf16[64,28,1024]{2,0,1:T(8,128)(2,1)}), bf16[64,28,512]{2,0,1:T(8,128)(2,1)}) %reduce-scatter.2.cloned.1.call-update) | async-done | bytes 1835024 | tf_op jit(solution)/shard_map/reduce_scatter | solution.py:25
  32.3 3.5 %gather_fusion = bf16[32,64,512]{2,1,0:T(8,128)(2,1)} fusion(bf16[64,28,512]{2,0,1:T(8,128)(2,1)} %reduce-scatter.2.cloned.1.call-done, s32[1024]{0:T(1024)S(1)} %pad_clamp_fusion.1), kind=kCustom, calls=%fused_computation | custom fusion | bytes 4194432 | tf_op jit(solution)/shard_map/jit(_take)/gather | solution.py:27
  35.8 1.9 select_bitcast_fusion
  37.7 53.8 %all_to_all.36 = bf16[64,32,512]{2,0,1:T(8,128)(2,1)S(1)} all-to-all(bf16[64,32,512]{2,0,1:T(8,128)(2,1)S(1)} %select_bitcast_fusion), channel_id=1, replica_groups=mesh['fsdp'=16,'dp'=2] {'fsdp'}, dimensions={1} | all-to-all | bytes 4194304 | tf_op jit(solution)/shard_map/all_to_all | solution.py:29
  91.5 1.5 copy.32
  93.0 0.0 all-gather.4.cloned.1.call-update
  93.0 0.0 all-gather.8.cloned.1.call-start
  93.0 0.0 all-gather.6.cloned.1.call-done
  93.1 14.0 %all-gather.4.cloned.1.call-done = bf16[1024,2,1024]{2,0,1:T(8,128)(2,1)} async-done(((bf16[1024,2,512]{2,0,1:T(8,128)(2,1)}), bf16[1024,2,1024]{2,0,1:T(8,128)(2,1)}) %all-gather.4.cloned.1.call-update) | async-done | bytes 4194320 | tf_op jit(solution)/shard_map/all_gather | solution.py:30
  107.0 0.0 copy-done
  107.0 10.4 %multiply_reduce_fusion = (f32[2]{0:T(128)S(1)}, f32[2,512,1024]{2,1,0:T(8,128)}) fusion(bf16[2,1024,1024]{2,1,0:T(8,128)(2,1)} %all-gather.6.cloned.1.call-done, bf16[1024,2,1024]{2,0,1:T(8,128)(2,1)} %all-gather.4.cloned.1.call-done, bf16[2,512,1024]{2,1,0:T(8,128)(2,1)S(1)} %copy-done), kind=kOutput, calls=%fused_computation.3 | convolution fusion | flops 4298113024 | bytes 14680072 | tf_op jit(solution)/shard_map/rjc,jck->rjk/dot_general | solution.py:43
  117.5 2.6 psum.7
  120.1 4.1 %fusion = bf16[512,2,1024]{2,0,1:T(8,128)(2,1)} fusion(f32[2,512,1024]{2,1,0:T(8,128)} %get-tuple-element.4, f32[2]{0:T(128)S(1)} %add_rsqrt_fusion), kind=kLoop, calls=%fused_computation.5 | loop fusion | flops 2097152 | bytes 6291464 | tf_op jit(solution)/shard_map/convert_element_type | solution.py:48
  124.2 0.0 all-gather.8.cloned.1.call-update
  124.3 15.0 %all-gather.8.cloned.1.call-done = bf16[1024,2,1024]{2,0,1:T(8,128)(2,1)} async-done(((bf16[512,2,1024]{2,0,1:T(8,128)(2,1)}), bf16[1024,2,1024]{2,0,1:T(8,128)(2,1)}) %all-gather.8.cloned.1.call-update) | async-done | bytes 4194320 | tf_op jit(solution)/shard_map/all_gather | solution.py:49
  139.3 8.5 %copy.36 = bf16[1024,2,1024]{2,1,0:T(2,128)(2,1)} copy(bf16[1024,2,1024]{2,0,1:T(8,128)(2,1)} %all-gather.8.cloned.1.call-done) | data formatting | bytes 8388608 | tf_op jit(solution)/shard_map/all_gather | solution.py:49
  147.7 7.0 %all-to-all-start.1 = ((bf16[1024,2,1024]{2,1,0:T(2,128)(2,1)}), bf16[1024,2,1024]{2,1,0:T(2,128)(2,1)}, u32[]{:S(2)}, u32[]{:S(2)}) async-start(bf16[1024,2,1024]{2,1,0:T(2,128)(2,1)} %copy.36), calls=%async_computation.2 | async-start | bytes 8388608 | tf_op jit(solution)/shard_map/all_to_all | solution.py:50
  154.7 0.1 broadcast_in_dim.61
  154.8 0.1 broadcast_in_dim.62
  154.9 0.0 copy-start.2
  154.9 0.0 copy-start.3
  154.9 8.6 %fusion.8 = f32[2,512,1024]{2,1,0:T(8,128)} fusion(f32[2,512,1024]{2,1,0:T(8,128)} %param.8, bf16[1024,2,1024]{2,0,1:T(8,128)(2,1)} %all-gather.4.cloned.1.call-done, s32[]{:T(128)S(6)} %select_n.47), kind=kOutput, calls=%fused_computation.14 | convolution fusion | flops 2148532224 | bytes 14680068 | tf_op jit(solution)/shard_map/rjc,kjc->jrk/dot_general | solution.py:33
  163.5 0.0 copy-done.2
  163.5 0.0 copy-done.3
  163.5 4.5 %fusion.11 = f32[2,512,1024]{2,1,0:T(8,128)} fusion(f32[2,512,1024]{2,1,0:T(8,128)S(1)} %copy-done.2, bf16[1024,2,1024]{2,0,1:T(8,128)(2,1)S(1)} %copy-done.3, s32[]{:T(128)S(6)} %select_n.47), kind=kOutput, calls=%fused_computation.15 | convolution fusion | flops 2148532224 | bytes 14680068 | tf_op jit(solution)/shard_map/rjc,rjk->jck/dot_general | solution.py:37
  167.9 82.6 %all-to-all-done.1 = bf16[1024,2,1024]{2,1,0:T(2,128)(2,1)} async-done(((bf16[1024,2,1024]{2,1,0:T(2,128)(2,1)}), bf16[1024,2,1024]{2,1,0:T(2,128)(2,1)}, u32[]{:S(2)}, u32[]{:S(2)}) %all-to-all-start.1) | async-done | bytes 4194336 | tf_op jit(solution)/shard_map/all_to_all | solution.py:50
  250.5 3.5 %copy.37 = bf16[1024,2,1024]{2,0,1:T(8,128)(2,1)S(1)} copy(bf16[1024,2,1024]{2,1,0:T(2,128)(2,1)} %all-to-all-done.1) | data formatting | bytes 8388608 | tf_op jit(solution)/shard_map/all_to_all | solution.py:50
  254.0 2.4 copy.38
  256.4 4.9 %gather_fusion.1 = bf16[28,64,1024]{2,1,0:T(8,128)(2,1)} fusion(bf16[64,32,1024]{2,0,1:T(8,128)(2,1)} %bitcast.30, s32[1024]{0:T(1024)S(1)} %pad_clamp_fusion), kind=kCustom, calls=%fused_computation.1 | custom fusion | bytes 7340144 | tf_op jit(solution)/shard_map/jit(_take)/gather | solution.py:51
  261.2 0.0 copy-start.1
  261.2 2.6 copy.43
  263.8 2.6 broadcast_select_fusion
  266.3 0.0 copy-done.1
  (7 shorter events, 0.0 us)
Async XLA Ops:
  7.2 99.9 %copy-start = (bf16[2,512,1024]{2,1,0:T(8,128)(2,1)S(1)}, bf16[2,512,1024]{2,1,0:T(8,128)(2,1)}, u32[]{:S(2)}) copy-start(bf16[2,512,1024]{2,1,0:T(8,128)(2,1)} %param.10) | copy-start | bytes 6291460
  7.2 25.1 %reduce-scatter.2.cloned.1.call-start = ((), (), s32[]{:S(2)}) async-start(), calls=%async_computation.3 | async-start | bytes 5505024 | tf_op jit(solution)/shard_map/reduce_scatter | solution.py:25
  19.0 0.8 copy-start.4
  19.0 74.0 %all-gather.6.cloned.1.call-start = ((), (), s32[]{:S(2)}) async-start(), calls=%async_computation.5 | async-start | bytes 6291456 | tf_op jit(solution)/shard_map/all_gather | solution.py:32
  19.8 87.3 %all-gather.4.cloned.1.call-start = ((), (), s32[]{:S(2)}) async-start(), calls=%async_computation.4 | async-start | bytes 6291456 | tf_op jit(solution)/shard_map/all_gather | solution.py:30
  93.0 46.3 %all-gather.8.cloned.1.call-start = ((), (), s32[]{:S(2)}) async-start(), calls=%async_computation.6 | async-start | bytes 6291456 | tf_op jit(solution)/shard_map/all_gather | solution.py:49
  147.7 102.8 %all-to-all-start.1 = ((bf16[1024,2,1024]{2,1,0:T(2,128)(2,1)}), bf16[1024,2,1024]{2,1,0:T(2,128)(2,1)}, u32[]{:S(2)}, u32[]{:S(2)}) async-start(bf16[1024,2,1024]{2,1,0:T(2,128)(2,1)} %copy.36), calls=%async_computation.2 | async-start | bytes 8388608 | tf_op jit(solution)/shard_map/all_to_all | solution.py:50
  154.9 8.6 %copy-start.2 = (f32[2,512,1024]{2,1,0:T(8,128)S(1)}, f32[2,512,1024]{2,1,0:T(8,128)}, u32[]{:S(2)}) copy-start(f32[2,512,1024]{2,1,0:T(8,128)} %param.9) | copy-start | bytes 12582916
  154.9 8.6 %copy-start.3 = (bf16[1024,2,1024]{2,0,1:T(8,128)(2,1)S(1)}, bf16[1024,2,1024]{2,0,1:T(8,128)(2,1)}, u32[]{:S(2)}) copy-start(bf16[1024,2,1024]{2,0,1:T(8,128)(2,1)} %all-gather.4.cloned.1.call-done) | copy-start | bytes 12582916
  261.2 5.1 %copy-start.1 = (bf16[2,512,1024]{2,1,0:T(8,128)(2,1)S(1)}, bf16[2,512,1024]{2,1,0:T(8,128)(2,1)}, u32[]{:S(2)}) copy-start(bf16[2,512,1024]{2,1,0:T(8,128)(2,1)} %param.10) | copy-start | bytes 6291460
Sparse Core Ops, SparseCore 0:
  19.1 13.0 reduce-scatter.1
  33.8 14.8 all-gather.5
  93.1 13.8 all-gather.3
  124.4 14.8 all-gather.7
where the time goes:
time: 273 us
  waiting for transfers between devices  124 us (45%)
  blocking collectives  56.4 us (21%)
  local copies, waits for them, and re-layouts  38.6 us (14%)
  matrix products  23.5 us (9%)
  between operations  13.9 us (5%)
  other arithmetic  8.9 us (3%)
  starting transfers between devices  7.12 us (3%)
    all_to_all x1, waiting for transfers between devices, per_device(): lax.all_to_all(full_rows, 'fsdp', split_axis=0, concat_axis=1, tiled=True)  82.6 us
    all_to_all x1, blocking collectives, per_device(): lax.all_to_all(outgoing, 'fsdp', split_axis=1, concat_axis=0, tiled=True)  53.8 us
    all_gather x1, waiting for transfers between devices, per_device(): full_rows = lax.all_gather(scaled, 'dp', axis=0, tiled=True)  15 us
    all_gather x1, waiting for transfers between devices, per_device(): gradient = lax.all_gather(incoming, 'dp', axis=2, tiled=True)  14 us
    reduce_scatter x1, waiting for transfers between devices, per_device(): lax.psum_scatter(band.astype(jnp.bfloat16), 'dp', scatter_dimension=2, ti...  12.2 us
    squeeze x2, local copies, waits for them, and re-layouts, per_device(): local_rows = grads[0]  11.7 us
    dot_general x1, matrix products, per_device(): jnp.einsum('rjc,jck->rjk', left_applied, whole_right, preferred_element_t...  10.4 us
    dot_general x1, matrix products, per_device(): jnp.einsum('rjc,kjc->jrk', own_rows, gradient, preferred_element_type=jnp...  8.58 us
  transfers between devices with their start and end apart: 5, of which 4 were waited for; matrix products, arithmetic and copies ran while one was open for 7% of the time, Pallas kernels for 0%

commit v1 on v0

--- a/solution.py
+++ b/solution.py
@@ -1,9 +1,468 @@
+import functools
 import jax
 import jax.numpy as jnp
 from jax import lax
+from jax.experimental import pallas as pl
+from jax.experimental.pallas import tpu as pltpu
 from jax.sharding import PartitionSpec as P
 
 epsilon = 1e-06
+VMEM_BYTES = 60 * 1024 * 1024
+
+
+def exchange_kernel(
+    sizes,
+    source_ref,
+    grads_hbm,
+    left_hbm,
+    right_hbm,
+    gradient_out,
+    returned_out,
+    factor_out,
+    grads,
+    outgoing,
+    incoming,
+    summed,
+    gradient,
+    left,
+    right,
+    total,
+    applied,
+    factor,
+    load_sem,
+    local_sem,
+    root_send,
+    root_recv,
+    swap_send,
+    swap_recv,
+    there_send,
+    there_recv,
+    back_send,
+    back_recv,
+    relay_send,
+    relay_recv,
+    factor_send,
+    factor_recv,
+    whole_send,
+    whole_recv,
+):
+    owners, cores, rows, size, group = sizes
+    groups = owners // group
+    depth = group * rows
+    half = size // cores
+    me = lax.axis_index("fsdp")
+    core = lax.axis_index("dp")
+    other = 1 - core
+    my_group = me // group
+    my_place = me % group
+    far_first = [groups // 2] + [d for d in range(groups - 1, 0, -1) if d != groups // 2] + [0]
+    near_first = [0] + far_first[:-1]
+
+    def target(shift, step):
+        return ((my_group + shift) % groups) * group + (my_place + step) % group
+
+    def origin(shift, step):
+        return ((my_group + groups - shift) % groups) * group + (my_place + group - step) % group
+
+    def block_rows(device):
+        return pl.ds(pl.multiple_of(device * rows, rows), rows)
+
+    def chosen(slot):
+        return grads[source_ref[slot]]
+
+    def remote(src, dst, send, recv, owner, to_core):
+        return pltpu.make_async_remote_copy(
+            src_ref=src,
+            dst_ref=dst,
+            send_sem=send,
+            recv_sem=recv,
+            device_id={"fsdp": owner, "dp": to_core},
+            device_id_type=pl.DeviceIdType.MESH,
+        )
+
+    def load(block, carry):
+        columns = pl.ds(pl.multiple_of(block * size, size), size)
+        pltpu.make_async_copy(grads_hbm.at[0, :, columns], grads.at[block], load_sem).start()
+        return carry
+
+    lax.fori_loop(0, grads.shape[0], load, 0)
+    barrier = pltpu.get_barrier_semaphore()
+    pl.semaphore_signal(
+        barrier,
+        inc=1,
+        device_id={"fsdp": me, "dp": other},
+        device_id_type=pl.DeviceIdType.MESH,
+    )
+
+    def greet(step, carry):
+        pl.semaphore_signal(
+            barrier,
+            inc=1,
+            device_id={"fsdp": (me + step) % owners, "dp": core},
+            device_id_type=pl.DeviceIdType.MESH,
+        )
+        return carry
+
+    lax.fori_loop(1, owners, greet, 0)
+    own_half = pl.ds(pl.multiple_of(core * half, half), half)
+    other_half = pl.ds(pl.multiple_of(other * half, half), half)
+    keep_left = pltpu.make_async_copy(left_hbm.at[core], left.at[own_half], local_sem.at[0])
+    keep_right = pltpu.make_async_copy(right_hbm.at[core], right.at[own_half], local_sem.at[1])
+    keep_left.start()
+    keep_right.start()
+    pltpu.make_async_copy(grads, grads, load_sem).wait()
+
+    def pick(device, carry):
+        outgoing[device] = chosen(device * cores + other)
+        return carry
+
+    lax.fori_loop(0, owners, pick, 0)
+    pl.semaphore_wait(barrier, owners)
+
+    def swap(device, index):
+        return remote(
+            outgoing.at[device],
+            incoming.at[device],
+            swap_send.at[index],
+            swap_recv.at[index],
+            me,
+            other,
+        )
+
+    for order, shift in enumerate(far_first):
+
+        def start_swap(step, carry):
+            swap(target(shift, step), order * group + step).start()
+            return carry
+
+        lax.fori_loop(0, group, start_swap, 0)
+
+    give_left = remote(
+        left_hbm.at[other], left.at[own_half], root_send.at[0], root_recv.at[0], me, other
+    )
+    give_right = remote(
+        right_hbm.at[other], right.at[own_half], root_send.at[1], root_recv.at[1], me, other
+    )
+    give_left.start()
+    give_right.start()
+
+    def there(device, index):
+        return remote(
+            summed.at[device],
+            gradient.at[block_rows(me)],
+            there_send.at[index],
+            there_recv.at[index],
+            device,
+            core,
+        )
+
+    def summed_block(device, index):
+        mine = chosen(device * cores + core)
+        swap(device, index).wait_recv()
+        return (mine.astype(jnp.float32) + incoming[device].astype(jnp.float32)).astype(
+            jnp.bfloat16
+        )
+
+    for order, shift in enumerate(far_first):
+
+        def start_there(step, carry):
+            device = target(shift, step)
+            index = order * group + step
+            summed[device] = summed_block(device, index)
+            there(device, index).start()
+            return carry
+
+        lax.fori_loop(0 if shift else 1, group, start_there, 0)
+    gradient[block_rows(me)] = summed_block(me, (groups - 1) * group)
+
+    keep_left.wait()
+    keep_right.wait()
+    give_left.wait_recv()
+    give_right.wait_recv()
+
+    def wait_there(shift):
+        order = far_first.index(shift)
+
+        def body(step, carry):
+            there(me, order * group + step).wait_recv()
+            return carry
+
+        lax.fori_loop(0 if shift else 1, group, body, 0)
+
+    def group_rows(index):
+        return pl.ds(pl.multiple_of(index * depth, depth), depth)
+
+    for order, shift in enumerate(near_first[:-1]):
+        wait_there(shift)
+        deep = group_rows((my_group + groups - shift) % groups)
+
+        def accumulate(index, carry):
+            part = jnp.dot(
+                left[group_rows(index), deep],
+                gradient[deep],
+                preferred_element_type=jnp.float32,
+            )
+            if order:
+                part = part + total[group_rows(index)]
+            total[group_rows(index)] = part
+            return carry
+
+        lax.fori_loop(0, groups, accumulate, 0)
+
+    wait_there(near_first[-1])
+    deep = group_rows((my_group + groups - near_first[-1]) % groups)
+
+    def back(device, index):
+        return remote(
+            applied.at[block_rows(device)],
+            returned_out.at[core, me],
+            back_send.at[index],
+            back_recv.at[index],
+            device,
+            core,
+        )
+
+    squares = jnp.zeros((1, size), jnp.float32)
+    for order, shift in enumerate(far_first):
+        out_rows = group_rows((my_group + shift) % groups)
+        left_applied = jnp.dot(
+            left[out_rows, deep], gradient[deep], preferred_element_type=jnp.float32
+        )
+        left_applied = (left_applied + total[out_rows]).astype(jnp.bfloat16)
+        both = jnp.dot(left_applied, right[...], preferred_element_type=jnp.float32)
+        squares = squares + jnp.sum(both * both, axis=0, keepdims=True)
+        applied[out_rows] = both.astype(jnp.bfloat16)
+
+        def start_back(step, carry):
+            back(target(shift, step), order * group + step).start()
+            return carry
+
+        lax.fori_loop(0 if shift else 1, group, start_back, 0)
+
+    scale = lax.rsqrt(jnp.sum(squares, axis=1, keepdims=True) / (size * size) + epsilon)
+    factor[...] = jnp.broadcast_to(scale, factor.shape)
+
+    def give_factor(device, index):
+        return remote(
+            factor,
+            factor_out.at[core, me],
+            factor_send.at[index],
+            factor_recv.at[index],
+            device,
+            core,
+        )
+
+    def start_factor(step, carry):
+        give_factor((me + step) % owners, step).start()
+        return carry
+
+    lax.fori_loop(1, owners, start_factor, 0)
+    keep_factor = pltpu.make_async_copy(factor, factor_out.at[core, me], local_sem.at[0])
+    keep_factor.start()
+    keep_gradient = pltpu.make_async_copy(gradient, gradient_out.at[core], local_sem.at[1])
+    keep_gradient.start()
+    keep_back = pltpu.make_async_copy(
+        applied.at[block_rows(me)], returned_out.at[core, me], local_sem.at[2]
+    )
+    keep_back.start()
+    own_relay = remote(
+        applied.at[block_rows(me)],
+        returned_out.at[core, me],
+        relay_send.at[(groups - 1) * group],
+        relay_recv.at[(groups - 1) * group],
+        me,
+        other,
+    )
+    own_relay.start()
+    give_gradient = remote(
+        gradient, gradient_out.at[core], whole_send.at[0], whole_recv.at[0], me, other
+    )
+    give_gradient.start()
+
+    def relay(device, index):
+        return remote(
+            returned_out.at[core, device],
+            returned_out.at[core, device],
+            relay_send.at[index],
+            relay_recv.at[index],
+            me,
+            other,
+        )
+
+    for shift in near_first:
+        order = far_first.index(shift)
+
+        def start_relay(step, carry):
+            index = order * group + step
+            back(me, index).wait_recv()
+            relay(origin(shift, step), index).start()
+            return carry
+
+        lax.fori_loop(0 if shift else 1, group, start_relay, 0)
+
+    def wait_factor(step, carry):
+        give_factor(me, step).wait_recv()
+        return carry
+
+    lax.fori_loop(1, owners, wait_factor, 0)
+    keep_factor.wait()
+    whole_factor = remote(
+        factor_out.at[core], factor_out.at[core], whole_send.at[1], whole_recv.at[1], me, other
+    )
+    whole_factor.start()
+
+    def drain(index, carry):
+        swap(me, index).wait_send()
+        relay(me, index).wait()
+        return carry
+
+    lax.fori_loop(0, owners, drain, 0)
+
+    def drain_far(index, carry):
+        there(me, index).wait_send()
+        back(me, index).wait_send()
+        return carry
+
+    lax.fori_loop(0, (groups - 1) * group, drain_far, 0)
+    lax.fori_loop((groups - 1) * group + 1, owners, drain_far, 0)
+
+    def drain_factor(step, carry):
+        give_factor(me, step).wait_send()
+        return carry
+
+    lax.fori_loop(1, owners, drain_factor, 0)
+    give_left.wait_send()
+    give_right.wait_send()
+    keep_gradient.wait()
+    keep_back.wait()
+    give_gradient.wait()
+    whole_factor.wait()
+
+
+def exchange(source, grads, left_root, right_root):
+    slots, half, size = left_root.shape
+    rows = grads.shape[1]
+    owners = lax.axis_size("fsdp")
+    cores = lax.axis_size("dp")
+    group = max(1, min(owners, 256 // rows))
+    dma = pltpu.SemaphoreType.DMA
+    bf16 = jnp.bfloat16
+    anywhere = pl.BlockSpec(memory_space=pl.ANY)
+    return pl.pallas_call(
+        functools.partial(exchange_kernel, (owners, cores, rows, size, group)),
+        out_shape=(
+            jax.ShapeDtypeStruct((cores, size, size), bf16),
+            jax.ShapeDtypeStruct((cores, owners, rows, size), bf16),
+            jax.ShapeDtypeStruct((cores, owners, 8, 128), jnp.float32),
+        ),
+        in_specs=[pl.BlockSpec(memory_space=pltpu.SMEM)] + [anywhere] * 3,
+        out_specs=(anywhere,) * 3,
+        scratch_shapes=[
+            pltpu.VMEM((grads.shape[2] // size, rows, size), bf16),
+            pltpu.VMEM((owners, rows, size), bf16),
+            pltpu.VMEM((owners, rows, size), bf16),
+            pltpu.VMEM((owners, rows, size), bf16),
+            pltpu.VMEM((size, size), bf16),
+            pltpu.VMEM((size, size), bf16),
+            pltpu.VMEM((size, size), bf16),
+            pltpu.VMEM((size, size), jnp.float32),
+            pltpu.VMEM((size, size), bf16),
+            pltpu.VMEM((8, 128), jnp.float32),
+            dma,
+            dma((3,)),
+            dma((2,)),
+            dma((2,)),
+        ]
+        + [dma((owners,))] * 10
+        + [dma((2,)), dma((2,))],
+        compiler_params=pltpu.CompilerParams(
+            collective_id=0, has_side_effects=True, vmem_limit_bytes=VMEM_BYTES
+        ),
+    )(source, grads, left_root, right_root)
+
+
+def statistics_kernel(tile, place_ref, filled_ref, gradient, left_in, right_in, left_out, right_out):
+    size = gradient.shape[1]
+    start = place_ref[0] * left_in.shape[1] * pl.num_programs(1) + pl.program_id(1) * tile
+    part = pl.ds(pl.multiple_of(start, tile), tile)
+    filled = filled_ref[place_ref[1] + pl.program_id(0)] > 0
+    left_gram = lax.dot_general(
+        gradient[0, part, :],
+        gradient[0],
+        (((1,), (1,)), ((), ())),
+        preferred_element_type=jnp.float32,
+    )
+    left_out[0] = left_in[0] + jnp.where(filled, left_gram, 0.0)
+    right_gram = lax.dot_general(
+        gradient[0, :, part],
+        gradient[0],
+        (((0,), (0,)), ((), ())),
+        preferred_element_type=jnp.float32,
+    )
+    right_out[0] = right_in[0] + jnp.where(filled, right_gram, 0.0)
+
+
+def statistics(filled, gradient, left_stats, right_stats):
+    slots, half, size = left_stats.shape
+    tile = min(half, 256)
+    place = jnp.stack([lax.axis_index("dp"), lax.axis_index("fsdp") * slots]).astype(jnp.int32)
+    whole = pl.BlockSpec((1, size, size), lambda s, r, p, f: (s, 0, 0))
+    band = pl.BlockSpec((1, tile, size), lambda s, r, p, f: (s, r, 0))
+    out = jax.ShapeDtypeStruct(left_stats.shape, jnp.float32)
+    return pl.pallas_call(
+        functools.partial(statistics_kernel, tile),
+        out_shape=(out, out),
+        grid_spec=pltpu.PrefetchScalarGridSpec(
+            num_scalar_prefetch=2,
+            grid=(slots, half // tile),
+            in_specs=[whole, band, band],
+            out_specs=(band, band),
+        ),
+        compiler_params=pltpu.CompilerParams(vmem_limit_bytes=VMEM_BYTES),
+    )(place, filled, gradient, left_stats, right_stats)
+
+
+def assemble_kernel(count, slot_ref, returned, factor, update):
+    cores, size = returned.shape[0], returned.shape[3]
+    for index in range(count):
+        slot = slot_ref[pl.program_id(0) * count + index]
+        owner, core = slot // cores, slot % cores
+        scale = factor[core, owner][:1, :1]
+        piece = returned[core, owner].astype(jnp.float32) * scale
+        update[:, index * size : (index + 1) * size] = piece.astype(update.dtype)
+
+
+def assemble(block_slot, returned, factor):
+    cores, owners, rows, size = returned.shape
+    blocks = block_slot.shape[0]
+    steps = next(n for n in (4, 2, 1) if blocks % n == 0)
+    count = blocks // steps
+    return pl.pallas_call(
+        functools.partial(assemble_kernel, count),
+        out_shape=jax.ShapeDtypeStruct((rows, blocks * size), returned.dtype),
+        grid_spec=pltpu.PrefetchScalarGridSpec(
+            num_scalar_prefetch=1,
+            grid=(steps,),
+            in_specs=[
+                pl.BlockSpec(returned.shape, lambda i, s: (0, 0, 0, 0)),
+                pl.BlockSpec(factor.shape, lambda i, s: (0, 0, 0, 0)),
+            ],
+            out_specs=pl.BlockSpec((rows, count * size), lambda i, s: (0, i)),
+        ),
+        compiler_params=pltpu.CompilerParams(vmem_limit_bytes=VMEM_BYTES),
+    )(block_slot, returned, factor)
+
+
+def slot_per_core(grads, block_slot, left_stats, right_stats, left_root, right_root):
+    block_count = block_slot.shape[0]
+    total_slots = left_stats.shape[0] * lax.axis_size("fsdp")
+    matches = block_slot[None, :] == jnp.arange(total_slots, dtype=jnp.int32)[:, None]
+    numbers = jnp.arange(block_count, dtype=jnp.int32)
+    source = jnp.sum(jnp.where(matches, numbers[None, :], 0), axis=1)
+    filled = jnp.sum(matches.astype(jnp.int32), axis=1)
+    gradient, returned, factor = exchange(source, grads, left_root, right_root)
+    left_new, right_new = statistics(filled, gradient, left_stats, right_stats)
+    return (left_new, right_new, assemble(block_slot, returned, factor))
 
 
 def per_device(grads, block_slot, left_stats, right_stats, left_root, right_root):
@@ -52,6 +511,16 @@
     return (left_new, right_new, update)
 
 
+def per_shard(*args):
+    grads, _, left_stats = args[:3]
+    slots, rows = left_stats.shape[0], grads.shape[1]
+    paired = slots == 2 and lax.axis_size("dp") == 2
+    even = rows % 16 == 0 and 256 % rows == 0 and lax.axis_size("fsdp") % (256 // rows) == 0
+    if paired and even:
+        return slot_per_core(*args)
+    return per_device(*args)
+
+
 def solution(mesh):
     in_specs = (
         P("dp", "fsdp", None),
@@ -63,5 +532,5 @@
     )
     out_specs = (P("fsdp", "dp", None), P("fsdp", "dp", None), P("fsdp", None))
     return jax.shard_map(
-        per_device, mesh=mesh, in_specs=in_specs, out_specs=out_specs, check_vma=False
-    )
+        per_shard, mesh=mesh, in_specs=in_specs, out_specs=out_specs, check_vma=False
+    )

time: 273 us -> 132 us (0.48)
  the two profiles are of different devices: /device:TPU:14 before, /device:TPU:0 now
where the time goes in v1:
time: 132 us
  Pallas kernels  130 us (98%)
  other arithmetic  1.97 us (1%)
    pallas_call x1, Pallas kernels, exchange(): pl.pallas_call(functools.partial(exchange_kernel, (owners, cores, rows, s...  113 us
    pallas_call x1, Pallas kernels, statistics(): pl.pallas_call(functools.partial(statistics_kernel, tile), out_shape=(out...  11.3 us
    pallas_call x1, Pallas kernels, assemble(): pl.pallas_call(functools.partial(assemble_kernel, count), out_shape=jax.S...  5.51 us

profile of v1, /device:TPU:0, one launch (start us, length us, event | category | flops | bytes accessed | tf_op | source)
XLA Modules:
  0.0 132.1 jit_solution(14527733337406978546)
XLA Ops:
  0.6 0.6 pad_add_fusion.place_ref
  1.3 1.3 select_reduce_fusion
  2.6 112.7 %shard_map.85 = (bf16[2,1024,1024]{2,1,0:T(8,128)(2,1)}, bf16[2,16,64,1024]{3,2,1,0:T(8,128)(2,1)}, f32[2,16,8,128]{3,2,1,0:T(8,128)}) custom-call(s32[32]{0:T(128)} %get-tuple-element.13.source_ref, bf16[1,64,28672]{2,1,0:T(8,128)(2,1)} %grads_hbm.1, bf16[2,512,1024]{2,1,0:T(8,128)(2,1)} %left_hbm.1, bf16[2,512,1024]{2,1,0:T(8,128)(2,1)} %right_hbm.1), custom_call_target="tpu_custom_call" | custom-call | tf_op jit(solution)/shard_map/pallas_call | solution.py:351
  115.3 5.5 %shard_map.87 = bf16[64,28672]{1,0:T(8,128)(2,1)} custom-call(s32[28]{0:T(128)} %slot_ref.1, bf16[2,16,64,1024]{3,2,1,0:T(8,128)(2,1)} %get-tuple-element.11.returned, f32[2,16,8,128]{3,2,1,0:T(8,128)} %get-tuple-element.12.factor), custom_call_target="tpu_custom_call" | custom-call | tf_op jit(solution)/shard_map/pallas_call | solution.py:440
  120.8 11.3 %shard_map.86 = (f32[2,512,1024]{2,1,0:T(8,128)}, f32[2,512,1024]{2,1,0:T(8,128)}) custom-call(s32[2]{0:T(128)} %pad_add_fusion.place_ref, s32[32]{0:T(128)} %get-tuple-element.14.filled_ref, bf16[2,1024,1024]{2,1,0:T(8,128)(2,1)} %get-tuple-element.8.gradient, f32[2,512,1024]{2,1,0:T(8,128)} %left_in.1, f32[2,512,1024]{2,1,0:T(8,128)} %right_in.1), custom_call_target="tpu_custom_call" | custom-call | tf_op jit(solution)/shard_map/pallas_call | solution.py:412

commit v2 on v1

--- a/solution.py
+++ b/solution.py
@@ -7,29 +7,35 @@
 from jax.sharding import PartitionSpec as P
 
 epsilon = 1e-06
-VMEM_BYTES = 60 * 1024 * 1024
+VMEM_BYTES = 44 * 1024 * 1024
+FINISH_BYTES = 28 * 1024 * 1024
 
 
 def exchange_kernel(
     sizes,
     source_ref,
+    filled_ref,
     grads_hbm,
     left_hbm,
     right_hbm,
-    gradient_out,
+    left_stats,
+    right_stats,
+    left_out,
+    right_out,
     returned_out,
     factor_out,
     grads,
     outgoing,
     incoming,
     summed,
-    gradient,
+    gradients,
     left,
     right,
     total,
     applied,
     factor,
     load_sem,
+    stats_sem,
     local_sem,
     root_send,
     root_recv,
@@ -53,6 +59,7 @@
     me = lax.axis_index("fsdp")
     core = lax.axis_index("dp")
     other = 1 - core
+    gradient = gradients.at[core]
     my_group = me // group
     my_place = me % group
     far_first = [groups // 2] + [d for d in range(groups - 1, 0, -1) if d != groups // 2] + [0]
@@ -110,6 +117,10 @@
     keep_right = pltpu.make_async_copy(right_hbm.at[core], right.at[own_half], local_sem.at[1])
     keep_left.start()
     keep_right.start()
+    read_left = pltpu.make_async_copy(left_stats, left_out, stats_sem.at[0])
+    read_right = pltpu.make_async_copy(right_stats, right_out, stats_sem.at[1])
+    read_left.start()
+    read_right.start()
     pltpu.make_async_copy(grads, grads, load_sem).wait()
 
     def pick(device, carry):
@@ -222,6 +233,8 @@
             core,
         )
 
+    give_gradient = remote(gradient, gradient, whole_send.at[0], whole_recv.at[0], me, other)
+    give_gradient.start()
     squares = jnp.zeros((1, size), jnp.float32)
     for order, shift in enumerate(far_first):
         out_rows = group_rows((my_group + shift) % groups)
@@ -259,8 +272,6 @@
     lax.fori_loop(1, owners, start_factor, 0)
     keep_factor = pltpu.make_async_copy(factor, factor_out.at[core, me], local_sem.at[0])
     keep_factor.start()
-    keep_gradient = pltpu.make_async_copy(gradient, gradient_out.at[core], local_sem.at[1])
-    keep_gradient.start()
     keep_back = pltpu.make_async_copy(
         applied.at[block_rows(me)], returned_out.at[core, me], local_sem.at[2]
     )
@@ -274,10 +285,36 @@
         other,
     )
     own_relay.start()
-    give_gradient = remote(
-        gradient, gradient_out.at[core], whole_send.at[0], whole_recv.at[0], me, other
-    )
-    give_gradient.start()
+    read_left.wait()
+    read_right.wait()
+
+    def grams(slot):
+        def tile(index, carry):
+            start = pl.multiple_of(index * depth, depth)
+            out_part = pl.ds(start, depth)
+            part = pl.ds(pl.multiple_of(core * half + start, depth), depth)
+            filled = jnp.full((depth, size), filled_ref[me * cores + slot], jnp.int32) > 0
+            left_gram = lax.dot_general(
+                gradients[slot, part, :],
+                gradients[slot],
+                (((1,), (1,)), ((), ())),
+                preferred_element_type=jnp.float32,
+            )
+            left_out[slot, out_part] += jnp.where(filled, left_gram, 0.0)
+            right_gram = lax.dot_general(
+                gradients[slot, :, part],
+                gradients[slot],
+                (((0,), (0,)), ((), ())),
+                preferred_element_type=jnp.float32,
+            )
+            right_out[slot, out_part] += jnp.where(filled, right_gram, 0.0)
+            return carry
+
+        lax.fori_loop(0, half // depth, tile, 0)
+
+    grams(core)
+    give_gradient.wait_recv()
+    grams(other)
 
     def relay(device, index):
         return remote(
@@ -333,42 +370,45 @@
     lax.fori_loop(1, owners, drain_factor, 0)
     give_left.wait_send()
     give_right.wait_send()
-    keep_gradient.wait()
     keep_back.wait()
-    give_gradient.wait()
+    give_gradient.wait_send()
     whole_factor.wait()
 
 
-def exchange(source, grads, left_root, right_root):
+def exchange(source, filled, grads, left_root, right_root, left_stats, right_stats):
     slots, half, size = left_root.shape
     rows = grads.shape[1]
     owners = lax.axis_size("fsdp")
     cores = lax.axis_size("dp")
     group = max(1, min(owners, 256 // rows))
     dma = pltpu.SemaphoreType.DMA
-    bf16 = jnp.bfloat16
+    bf16, f32 = jnp.bfloat16, jnp.float32
     anywhere = pl.BlockSpec(memory_space=pl.ANY)
+    inside = pl.BlockSpec(memory_space=pltpu.VMEM)
+    scalars = pl.BlockSpec(memory_space=pltpu.SMEM)
     return pl.pallas_call(
         functools.partial(exchange_kernel, (owners, cores, rows, size, group)),
         out_shape=(
-            jax.ShapeDtypeStruct((cores, size, size), bf16),
-            jax.ShapeDtypeStruct((cores, owners, rows, size), bf16),
-            jax.ShapeDtypeStruct((cores, owners, 8, 128), jnp.float32),
+            pltpu.VMEM(left_stats.shape, f32),
+            pltpu.VMEM(left_stats.shape, f32),
+            pltpu.VMEM((cores, owners, rows, size), bf16),
+            pltpu.VMEM((cores, owners, 8, 128), f32),
         ),
-        in_specs=[pl.BlockSpec(memory_space=pltpu.SMEM)] + [anywhere] * 3,
-        out_specs=(anywhere,) * 3,
+        in_specs=[scalars] * 2 + [anywhere] * 5,
+        out_specs=(inside,) * 4,
         scratch_shapes=[
             pltpu.VMEM((grads.shape[2] // size, rows, size), bf16),
             pltpu.VMEM((owners, rows, size), bf16),
             pltpu.VMEM((owners, rows, size), bf16),
             pltpu.VMEM((owners, rows, size), bf16),
+            pltpu.VMEM((cores, size, size), bf16),
             pltpu.VMEM((size, size), bf16),
             pltpu.VMEM((size, size), bf16),
+            pltpu.VMEM((size, size), f32),
             pltpu.VMEM((size, size), bf16),
-            pltpu.VMEM((size, size), jnp.float32),
-            pltpu.VMEM((size, size), bf16),
-            pltpu.VMEM((8, 128), jnp.float32),
+            pltpu.VMEM((8, 128), f32),
             dma,
+            dma((2,)),
             dma((3,)),
             dma((2,)),
             dma((2,)),
@@ -378,79 +418,56 @@
         compiler_params=pltpu.CompilerParams(
             collective_id=0, has_side_effects=True, vmem_limit_bytes=VMEM_BYTES
         ),
-    )(source, grads, left_root, right_root)
-
-
-def statistics_kernel(tile, place_ref, filled_ref, gradient, left_in, right_in, left_out, right_out):
-    size = gradient.shape[1]
-    start = place_ref[0] * left_in.shape[1] * pl.num_programs(1) + pl.program_id(1) * tile
-    part = pl.ds(pl.multiple_of(start, tile), tile)
-    filled = filled_ref[place_ref[1] + pl.program_id(0)] > 0
-    left_gram = lax.dot_general(
-        gradient[0, part, :],
-        gradient[0],
-        (((1,), (1,)), ((), ())),
-        preferred_element_type=jnp.float32,
-    )
-    left_out[0] = left_in[0] + jnp.where(filled, left_gram, 0.0)
-    right_gram = lax.dot_general(
-        gradient[0, :, part],
-        gradient[0],
-        (((0,), (0,)), ((), ())),
-        preferred_element_type=jnp.float32,
-    )
-    right_out[0] = right_in[0] + jnp.where(filled, right_gram, 0.0)
-
-
-def statistics(filled, gradient, left_stats, right_stats):
-    slots, half, size = left_stats.shape
-    tile = min(half, 256)
-    place = jnp.stack([lax.axis_index("dp"), lax.axis_index("fsdp") * slots]).astype(jnp.int32)
-    whole = pl.BlockSpec((1, size, size), lambda s, r, p, f: (s, 0, 0))
-    band = pl.BlockSpec((1, tile, size), lambda s, r, p, f: (s, r, 0))
-    out = jax.ShapeDtypeStruct(left_stats.shape, jnp.float32)
-    return pl.pallas_call(
-        functools.partial(statistics_kernel, tile),
-        out_shape=(out, out),
-        grid_spec=pltpu.PrefetchScalarGridSpec(
-            num_scalar_prefetch=2,
-            grid=(slots, half // tile),
-            in_specs=[whole, band, band],
-            out_specs=(band, band),
-        ),
-        compiler_params=pltpu.CompilerParams(vmem_limit_bytes=VMEM_BYTES),
-    )(place, filled, gradient, left_stats, right_stats)
-
-
-def assemble_kernel(count, slot_ref, returned, factor, update):
+    )(source, filled, grads, left_root, right_root, left_stats, right_stats)
+
+
+def finish_kernel(
+    steps, slot_ref, left, right, returned, factor, left_out, right_out, update_out, update, sems
+):
     cores, size = returned.shape[0], returned.shape[3]
-    for index in range(count):
-        slot = slot_ref[pl.program_id(0) * count + index]
-        owner, core = slot // cores, slot % cores
-        scale = factor[core, owner][:1, :1]
-        piece = returned[core, owner].astype(jnp.float32) * scale
-        update[:, index * size : (index + 1) * size] = piece.astype(update.dtype)
-
-
-def assemble(block_slot, returned, factor):
+    count = update.shape[1] // size // steps
+    copies = [
+        pltpu.make_async_copy(left, left_out, sems.at[0]),
+        pltpu.make_async_copy(right, right_out, sems.at[1]),
+    ]
+    copies[0].start()
+    copies[1].start()
+    for step in range(steps):
+        for index in range(step * count, (step + 1) * count):
+            slot = slot_ref[index]
+            owner, core = slot // cores, slot % cores
+            scale = factor[core, owner][:1, :1]
+            piece = returned[core, owner].astype(jnp.float32) * scale
+            update[:, index * size : (index + 1) * size] = piece.astype(update.dtype)
+        columns = pl.ds(step * count * size, count * size)
+        copy = pltpu.make_async_copy(
+            update.at[:, columns], update_out.at[:, columns], sems.at[2 + step]
+        )
+        copy.start()
+        copies.append(copy)
+    for copy in copies:
+        copy.wait()
+
+
+def finish(block_slot, left, right, returned, factor):
     cores, owners, rows, size = returned.shape
     blocks = block_slot.shape[0]
     steps = next(n for n in (4, 2, 1) if blocks % n == 0)
-    count = blocks // steps
+    anywhere = pl.BlockSpec(memory_space=pl.ANY)
+    inside = pl.BlockSpec(memory_space=pltpu.VMEM)
+    stats = jax.ShapeDtypeStruct(left.shape, left.dtype)
+    update = jax.ShapeDtypeStruct((rows, blocks * size), returned.dtype)
     return pl.pallas_call(
-        functools.partial(assemble_kernel, count),
-        out_shape=jax.ShapeDtypeStruct((rows, blocks * size), returned.dtype),
-        grid_spec=pltpu.PrefetchScalarGridSpec(
-            num_scalar_prefetch=1,
-            grid=(steps,),
-            in_specs=[
-                pl.BlockSpec(returned.shape, lambda i, s: (0, 0, 0, 0)),
-                pl.BlockSpec(factor.shape, lambda i, s: (0, 0, 0, 0)),
-            ],
-            out_specs=pl.BlockSpec((rows, count * size), lambda i, s: (0, i)),
-        ),
-        compiler_params=pltpu.CompilerParams(vmem_limit_bytes=VMEM_BYTES),
-    )(block_slot, returned, factor)
+        functools.partial(finish_kernel, steps),
+        out_shape=(stats, stats, update),
+        in_specs=[pl.BlockSpec(memory_space=pltpu.SMEM)] + [inside] * 4,
+        out_specs=(anywhere,) * 3,
+        scratch_shapes=[
+            pltpu.VMEM(update.shape, update.dtype),
+            pltpu.SemaphoreType.DMA((2 + steps,)),
+        ],
+        compiler_params=pltpu.CompilerParams(vmem_limit_bytes=FINISH_BYTES),
+    )(block_slot, left, right, returned, factor)
 
 
 def slot_per_core(grads, block_slot, left_stats, right_stats, left_root, right_root):
@@ -460,9 +477,10 @@
     numbers = jnp.arange(block_count, dtype=jnp.int32)
     source = jnp.sum(jnp.where(matches, numbers[None, :], 0), axis=1)
     filled = jnp.sum(matches.astype(jnp.int32), axis=1)
-    gradient, returned, factor = exchange(source, grads, left_root, right_root)
-    left_new, right_new = statistics(filled, gradient, left_stats, right_stats)
-    return (left_new, right_new, assemble(block_slot, returned, factor))
+    left, right, returned, factor = exchange(
+        source, filled, grads, left_root, right_root, left_stats, right_stats
+    )
+    return finish(block_slot, left, right, returned, factor)
 
 
 def per_device(grads, block_slot, left_stats, right_stats, left_root, right_root):

time: 132 us -> 120 us (0.909)
  Pallas kernels: 130 us -> 118 us
    pallas_call x2 -> x1, Pallas kernels: 16.9 us -> 5.23 us  [finish(): pl.pallas_call(functools.partial(finish_kernel, steps), out_shape=(stats,...]
where the time goes in v2:
time: 120 us
  Pallas kernels  118 us (98%)
  other arithmetic  1.29 us (1%)
    pallas_call x1, Pallas kernels, exchange(): pl.pallas_call(functools.partial(exchange_kernel, (owners, cores, rows, s...  112 us
    pallas_call x1, Pallas kernels, finish(): pl.pallas_call(functools.partial(finish_kernel, steps), out_shape=(stats,...  5.23 us

profile of v2, /device:TPU:0, one launch (start us, length us, event | category | flops | bytes accessed | tf_op | source)
XLA Modules:
  0.0 119.6 jit_solution(10136264918866208822)
XLA Ops:
  0.6 1.3 %convert_reduce_fusion = (s32[32]{0:T(128)}, s32[32]{0:T(128)}) fusion(s32[28]{0:T(128)} %slot_ref.1), kind=kLoop, calls=%fused_computation | loop fusion | flops 4416 | bytes 368 | tf_op jit(solution)/shard_map/reduce_sum | solution.py:479
  1.9 0.0 copy-start
  1.9 112.4 %shard_map.85 = (f32[2,512,1024]{2,1,0:T(8,128)S(1)}, f32[2,512,1024]{2,1,0:T(8,128)S(1)}, bf16[2,16,64,1024]{3,2,1,0:T(8,128)(2,1)S(1)}, f32[2,16,8,128]{3,2,1,0:T(8,128)S(1)}) custom-call(s32[32]{0:T(128)} %get-tuple-element.12.source_ref, s32[32]{0:T(128)} %get-tuple-element.11.filled_ref, bf16[1,64,28672]{2,1,0:T(8,128)(2,1)} %grads_hbm.1, ...), custom_call_target="tpu_custom_call" | custom-call | tf_op jit(solution)/shard_map/pallas_call | solution.py:389
  114.3 0.0 copy-done
  114.3 5.2 %shard_map.86 = (f32[2,512,1024]{2,1,0:T(8,128)}, f32[2,512,1024]{2,1,0:T(8,128)}, bf16[64,28672]{1,0:T(8,128)(2,1)}) custom-call(s32[28]{0:T(128)S(1)} %copy-done, f32[2,512,1024]{2,1,0:T(8,128)S(1)} %get-tuple-element.7.left, f32[2,512,1024]{2,1,0:T(8,128)S(1)} %get-tuple-element.8.right, bf16[2,16,64,1024]{3,2,1,0:T(8,128)(2,1)S(1)} %get-tuple-element.9.returned, ...), custom_call_target="tpu_custom_call" | custom-call | tf_op jit(solution)/shard_map/pallas_call | solution.py:460
Async XLA Ops:
  1.9 112.4 %copy-start = (s32[28]{0:T(128)S(1)}, s32[28]{0:T(128)}, u32[]{:S(2)}) copy-start(s32[28]{0:T(128)} %slot_ref.1) | copy-start | bytes 340

commit v3 on v2

--- a/solution.py
+++ b/solution.py
@@ -62,14 +62,18 @@
     gradient = gradients.at[core]
     my_group = me // group
     my_place = me % group
-    far_first = [groups // 2] + [d for d in range(groups - 1, 0, -1) if d != groups // 2] + [0]
+    far_first = [groups // 2] + [d for d in range(1, groups) if d != groups // 2] + [0]
     near_first = [0] + far_first[:-1]
 
+    def flipped(value, mask, count):
+        result, bit = 0, 1
+        while bit < count:
+            result = result + bit * ((value // bit + mask // bit) % 2)
+            bit = 2 * bit
+        return result
+
     def target(shift, step):
-        return ((my_group + shift) % groups) * group + (my_place + step) % group
-
-    def origin(shift, step):
-        return ((my_group + groups - shift) % groups) * group + (my_place + group - step) % group
+        return flipped(my_group, shift, groups) * group + flipped(my_place, step, group)
 
     def block_rows(device):
         return pl.ds(pl.multiple_of(device * rows, rows), rows)
@@ -205,7 +209,7 @@
 
     for order, shift in enumerate(near_first[:-1]):
         wait_there(shift)
-        deep = group_rows((my_group + groups - shift) % groups)
+        deep = group_rows(flipped(my_group, shift, groups))
 
         def accumulate(index, carry):
             part = jnp.dot(
@@ -221,7 +225,7 @@
         lax.fori_loop(0, groups, accumulate, 0)
 
     wait_there(near_first[-1])
-    deep = group_rows((my_group + groups - near_first[-1]) % groups)
+    deep = group_rows(flipped(my_group, near_first[-1], groups))
 
     def back(device, index):
         return remote(
@@ -237,7 +241,7 @@
     give_gradient.start()
     squares = jnp.zeros((1, size), jnp.float32)
     for order, shift in enumerate(far_first):
-        out_rows = group_rows((my_group + shift) % groups)
+        out_rows = group_rows(flipped(my_group, shift, groups))
         left_applied = jnp.dot(
             left[out_rows, deep], gradient[deep], preferred_element_type=jnp.float32
         )
@@ -332,7 +336,7 @@
         def start_relay(step, carry):
             index = order * group + step
             back(me, index).wait_recv()
-            relay(origin(shift, step), index).start()
+            relay(target(shift, step), index).start()
             return carry
 
         lax.fori_loop(0 if shift else 1, group, start_relay, 0)
@@ -534,7 +538,7 @@
     slots, rows = left_stats.shape[0], grads.shape[1]
     paired = slots == 2 and lax.axis_size("dp") == 2
     even = rows % 16 == 0 and 256 % rows == 0 and lax.axis_size("fsdp") % (256 // rows) == 0
-    if paired and even:
+    if paired and even and lax.axis_size("fsdp").bit_count() == 1:
         return slot_per_core(*args)
     return per_device(*args)
 

time: 120 us -> 120 us (level)
  no operation moved by 1% of the time
where the time goes in v3:
time: 120 us
  Pallas kernels  118 us (98%)
  other arithmetic  1.29 us (1%)
    pallas_call x1, Pallas kernels, exchange(): pl.pallas_call(functools.partial(exchange_kernel, (owners, cores, rows, s...  112 us
    pallas_call x1, Pallas kernels, finish(): pl.pallas_call(functools.partial(finish_kernel, steps), out_shape=(stats,...  5.23 us

profile of v3, /device:TPU:0, one launch (start us, length us, event | category | flops | bytes accessed | tf_op | source)
XLA Modules:
  0.0 119.6 jit_solution(8523868715664352897)
XLA Ops:
  0.6 1.3 %convert_reduce_fusion = (s32[32]{0:T(128)}, s32[32]{0:T(128)}) fusion(s32[28]{0:T(128)} %slot_ref.1), kind=kLoop, calls=%fused_computation | loop fusion | flops 4416 | bytes 368 | tf_op jit(solution)/shard_map/reduce_sum | solution.py:483
  1.9 0.0 copy-start
  1.9 112.4 %shard_map.85 = (f32[2,512,1024]{2,1,0:T(8,128)S(1)}, f32[2,512,1024]{2,1,0:T(8,128)S(1)}, bf16[2,16,64,1024]{3,2,1,0:T(8,128)(2,1)S(1)}, f32[2,16,8,128]{3,2,1,0:T(8,128)S(1)}) custom-call(s32[32]{0:T(128)} %get-tuple-element.12.source_ref, s32[32]{0:T(128)} %get-tuple-element.11.filled_ref, bf16[1,64,28672]{2,1,0:T(8,128)(2,1)} %grads_hbm.1, ...), custom_call_target="tpu_custom_call" | custom-call | tf_op jit(solution)/shard_map/pallas_call | solution.py:393
  114.4 0.0 copy-done
  114.4 5.2 %shard_map.86 = (f32[2,512,1024]{2,1,0:T(8,128)}, f32[2,512,1024]{2,1,0:T(8,128)}, bf16[64,28672]{1,0:T(8,128)(2,1)}) custom-call(s32[28]{0:T(128)S(1)} %copy-done, f32[2,512,1024]{2,1,0:T(8,128)S(1)} %get-tuple-element.7.left, f32[2,512,1024]{2,1,0:T(8,128)S(1)} %get-tuple-element.8.right, bf16[2,16,64,1024]{3,2,1,0:T(8,128)(2,1)S(1)} %get-tuple-element.9.returned, ...), custom_call_target="tpu_custom_call" | custom-call | tf_op jit(solution)/shard_map/pallas_call | solution.py:464
Async XLA Ops:
  1.9 112.5 %copy-start = (s32[28]{0:T(128)S(1)}, s32[28]{0:T(128)}, u32[]{:S(2)}) copy-start(s32[28]{0:T(128)} %slot_ref.1) | copy-start | bytes 340

commit v4 on v2

--- a/solution.py
+++ b/solution.py
@@ -87,12 +87,6 @@
             device_id_type=pl.DeviceIdType.MESH,
         )
 
-    def load(block, carry):
-        columns = pl.ds(pl.multiple_of(block * size, size), size)
-        pltpu.make_async_copy(grads_hbm.at[0, :, columns], grads.at[block], load_sem).start()
-        return carry
-
-    lax.fori_loop(0, grads.shape[0], load, 0)
     barrier = pltpu.get_barrier_semaphore()
     pl.semaphore_signal(
         barrier,
@@ -111,16 +105,17 @@
         return carry
 
     lax.fori_loop(1, owners, greet, 0)
+
+    def load(block, carry):
+        columns = pl.ds(pl.multiple_of(block * size, size), size)
+        pltpu.make_async_copy(grads_hbm.at[0, :, columns], grads.at[block], load_sem).start()
+        return carry
+
+    lax.fori_loop(0, grads.shape[0], load, 0)
     own_half = pl.ds(pl.multiple_of(core * half, half), half)
     other_half = pl.ds(pl.multiple_of(other * half, half), half)
     keep_left = pltpu.make_async_copy(left_hbm.at[core], left.at[own_half], local_sem.at[0])
     keep_right = pltpu.make_async_copy(right_hbm.at[core], right.at[own_half], local_sem.at[1])
-    keep_left.start()
-    keep_right.start()
-    read_left = pltpu.make_async_copy(left_stats, left_out, stats_sem.at[0])
-    read_right = pltpu.make_async_copy(right_stats, right_out, stats_sem.at[1])
-    read_left.start()
-    read_right.start()
     pltpu.make_async_copy(grads, grads, load_sem).wait()
 
     def pick(device, carry):
@@ -156,6 +151,8 @@
     )
     give_left.start()
     give_right.start()
+    keep_left.start()
+    keep_right.start()
 
     def there(device, index):
         return remote(
@@ -184,6 +181,10 @@
             return carry
 
         lax.fori_loop(0 if shift else 1, group, start_there, 0)
+    read_left = pltpu.make_async_copy(left_stats, left_out, stats_sem.at[0])
+    read_right = pltpu.make_async_copy(right_stats, right_out, stats_sem.at[1])
+    read_left.start()
+    read_right.start()
     gradient[block_rows(me)] = summed_block(me, (groups - 1) * group)
 
     keep_left.wait()

time: 120 us -> 119 us (level)
  no operation moved by 1% of the time
where the time goes in v4:
time: 119 us
  Pallas kernels  117 us (98%)
  other arithmetic  1.29 us (1%)
    pallas_call x1, Pallas kernels, exchange(): pl.pallas_call(functools.partial(exchange_kernel, (owners, cores, rows, s...  112 us
    pallas_call x1, Pallas kernels, finish(): pl.pallas_call(functools.partial(finish_kernel, steps), out_shape=(stats,...  5.23 us

profile of v4, /device:TPU:0, one launch (start us, length us, event | category | flops | bytes accessed | tf_op | source)
XLA Modules:
  0.0 119.3 jit_solution(12171121419715333437)
XLA Ops:
  0.6 1.3 %convert_reduce_fusion = (s32[32]{0:T(128)}, s32[32]{0:T(128)}) fusion(s32[28]{0:T(128)} %slot_ref.1), kind=kLoop, calls=%fused_computation | loop fusion | flops 4416 | bytes 368 | tf_op jit(solution)/shard_map/reduce_sum | solution.py:480
  1.9 0.0 copy-start
  1.9 112.1 %shard_map.85 = (f32[2,512,1024]{2,1,0:T(8,128)S(1)}, f32[2,512,1024]{2,1,0:T(8,128)S(1)}, bf16[2,16,64,1024]{3,2,1,0:T(8,128)(2,1)S(1)}, f32[2,16,8,128]{3,2,1,0:T(8,128)S(1)}) custom-call(s32[32]{0:T(128)} %get-tuple-element.12.source_ref, s32[32]{0:T(128)} %get-tuple-element.11.filled_ref, bf16[1,64,28672]{2,1,0:T(8,128)(2,1)} %grads_hbm.1, ...), custom_call_target="tpu_custom_call" | custom-call | tf_op jit(solution)/shard_map/pallas_call | solution.py:390
  114.1 0.0 copy-done
  114.1 5.2 %shard_map.86 = (f32[2,512,1024]{2,1,0:T(8,128)}, f32[2,512,1024]{2,1,0:T(8,128)}, bf16[64,28672]{1,0:T(8,128)(2,1)}) custom-call(s32[28]{0:T(128)S(1)} %copy-done, f32[2,512,1024]{2,1,0:T(8,128)S(1)} %get-tuple-element.7.left, f32[2,512,1024]{2,1,0:T(8,128)S(1)} %get-tuple-element.8.right, bf16[2,16,64,1024]{3,2,1,0:T(8,128)(2,1)S(1)} %get-tuple-element.9.returned, ...), custom_call_target="tpu_custom_call" | custom-call | tf_op jit(solution)/shard_map/pallas_call | solution.py:461
Async XLA Ops:
  1.9 112.1 %copy-start = (s32[28]{0:T(128)S(1)}, s32[28]{0:T(128)}, u32[]{:S(2)}) copy-start(s32[28]{0:T(128)} %slot_ref.1) | copy-start | bytes 340
